TPU v7x, 32 devices: a whole 2x2x4 slice. The times are simulated.
32 devices in a mesh: groups: 2 (over x), ctx: 4 (over y, core), heads: 4 (over z).
Axes of the slice: x: 2, y: 2, z: 4, core: 2. Of those that a mesh axis runs over, the one named last changes fastest.
Arguments:
- tokens: bfloat16 [4096, 2048], P(('groups', 'ctx', 'heads')), parts along dimension 0, may hold values from -60 to 60
- state_in: float32 [4, 256, 128], P('heads', 'groups'), parts along dimension 1, may hold values from -256 to 256
- past_kv: bfloat16 [2, 1024, 512], P(None, 'groups', 'heads'), parts along dimension 1, may hold values from -6 to 6
- w_qkv: bfloat16 [2048, 3, 512], P(None, None, 'heads'), may hold values from -0.125 to 0.125
- w_out: bfloat16 [512, 2048], P('heads'), may hold values from -0.25 to 0.25
- w_gate: bfloat16 [16, 2048, 768], P(('ctx', 'heads')), may hold values from -0.125 to 0.125
- w_up: bfloat16 [16, 2048, 768], P(('ctx', 'heads')), may hold values from -0.125 to 0.125
- w_down: bfloat16 [16, 768, 2048], P(('ctx', 'heads')), may hold values from -0.21875 to 0.21875
- expert_ids: int32 [4096, 8], P(('groups', 'ctx', 'heads')), parts along dimension 0, may hold values from 0 to 15, all different within a row; in each aligned block of 128 rows (0 to 127, 128 to 255, ...) at most 128 rows name the same one
- gate_weights: float32 [4096, 8], P(('groups', 'ctx', 'heads')), parts along dimension 0, may hold values from 0.1 to 1
Outputs:
- mixed: bfloat16 [4096, 2048], P(('groups', 'ctx', 'heads')), parts along dimension 0
There are 2 independent parts, one for each index of `groups`. A program takes and returns all parts, laid end to end along the dimension named above; an argument that names none is the same for every part. Nothing has to cross between parts.
Inputs may be any that keep to these rules, and one draw needn't show every extreme that they name: `expert_ids`: each row names 8 different experts; in each aligned block of 128 rows (the rows of one device) no expert is named by more than 128 rows, a bound that some block reaches.
All inputs are finite; a program needn't handle non-finite values.
Results may differ from a plain program's by a relative error of at most 0.017.
Values may be sent and summed in bfloat16 or wider, within the bound.
A program may use at most 128 MiB of HBM per device.

v0:
```python
import math
import jax
import jax.numpy as jnp
from jax import lax
from jax.sharding import PartitionSpec as P

HDIM = 128
WINDOW = 512


def entering(x, axis, join, neutral):
    place = lax.axis_index(axis)
    gathered = lax.all_gather(x.astype(jnp.bfloat16), axis)
    state = jnp.zeros_like(x) + jnp.asarray(neutral, x.dtype)

    def one(lap, state):
        return join(state, lax.dynamic_index_in_dim(gathered, lap, 0, False).astype(x.dtype))

    return lax.fori_loop(0, place, one, state)


def from_behind(block, axis, distance):
    devices = range(lax.axis_size(axis))
    route = [(i - distance, i) for i in devices if i - distance in devices]
    return lax.ppermute(block, axis, route)


def normalize(value):
    return value * lax.rsqrt(jnp.mean(value * value, axis=-1, keepdims=True) + 1e-06)


def dense_experts(
    hidden_float, normed, w_gate, w_up, w_down, expert_ids, gate_weights, expert_count
):
    axes = ("ctx", "heads")
    exp_local = w_gate.shape[0]
    chosen = expert_ids[:, :, None] == jnp.arange(expert_count, dtype=jnp.int32)
    table = jnp.sum(jnp.where(chosen, gate_weights[:, :, None], 0.0), axis=1)
    weights = lax.all_gather(table, axes, axis=0, tiled=True)
    first = lax.axis_index(axes) * exp_local
    rows = lax.all_gather(normed, axes, axis=0, tiled=True)
    total = None
    for e in range(exp_local):
        gate_act = jnp.dot(rows, w_gate[e], preferred_element_type=jnp.float32)
        up_act = jnp.dot(rows, w_up[e], preferred_element_type=jnp.float32)
        hid = (jax.nn.silu(gate_act) * up_act).astype(jnp.bfloat16)
        out_rows = jnp.dot(hid, w_down[e], preferred_element_type=jnp.float32)
        weight = lax.dynamic_slice_in_dim(weights, first + e, 1, 1)
        part = weight * out_rows
        total = part if total is None else total + part
    routed = lax.psum_scatter(total.astype(jnp.bfloat16), axes, scatter_dimension=0, tiled=True)
    return (hidden_float + routed.astype(jnp.float32)).astype(jnp.bfloat16)


def on_device(
    tokens, state_in, past_kv, w_qkv, w_out, w_gate, w_up, w_down, expert_ids, gate_weights
):
    row_count, model_width = tokens.shape
    inner_width = w_qkv.shape[2]
    local_heads = inner_width // HDIM
    w_flat = w_qkv.reshape(model_width, 3 * inner_width)
    projected = jnp.dot(
        lax.all_gather(tokens, "heads", axis=0, tiled=True),
        w_flat,
        preferred_element_type=jnp.float32,
    ).astype(jnp.bfloat16)
    slab_rows = projected.shape[0]
    projected = projected.reshape(slab_rows, 3, local_heads, HDIM)
    query = jnp.transpose(projected[:, 0], (1, 0, 2))
    keys = jnp.transpose(projected[:, 1], (1, 0, 2))
    values = jnp.transpose(projected[:, 2], (1, 0, 2))
    local_state = jnp.einsum("hsd,hse->hde", keys, values, preferred_element_type=jnp.float32)
    earlier_state = entering(
        local_state, "ctx", lambda first, second: first + second, jnp.zeros_like(local_state)
    )
    start_state = state_in + earlier_state
    tail = jnp.stack([keys, values], axis=0)
    arrived = from_behind(tail, "ctx", 1)
    past = jnp.transpose(past_kv.reshape(2, WINDOW, local_heads, HDIM), (0, 2, 1, 3))
    previous = jnp.where(lax.axis_index("ctx") == 0, past, arrived)
    all_keys = jnp.concatenate([previous[0], keys], axis=1)
    all_values = jnp.concatenate([previous[1], values], axis=1)
    block_rows = min(slab_rows, 512)
    block_count = slab_rows // block_rows
    scale = 1.0 / math.sqrt(HDIM)
    causal = jnp.arange(block_rows)[:, None] >= jnp.arange(block_rows)[None, :]
    offsets = jnp.arange(WINDOW + block_rows)[None, :] - jnp.arange(block_rows)[:, None]
    in_window = (offsets > 0) & (offsets <= WINDOW)

    def block_step(state, index):
        first = index * block_rows
        carried = jnp.einsum(
            "hsd,hde->hse", query.astype(jnp.float32), state, precision=lax.Precision.HIGHEST
        )
        inside = jnp.einsum("hsd,htd->hst", query, keys, preferred_element_type=jnp.float32)
        inside = jnp.where(causal[None], inside, 0.0).astype(jnp.bfloat16)
        linear = carried + jnp.einsum(
            "hst,hte->hse", inside, values, preferred_element_type=jnp.float32
        )
        scores = (
            jnp.einsum("hsd,htd->hst", query, all_keys, preferred_element_type=jnp.float32) * scale
        )
        scores = jnp.where(in_window[None], scores, -jnp.inf)
        top_score = jnp.max(scores, axis=-1, keepdims=True)
        expo = jnp.exp(scores - top_score)
        probs = (expo / jnp.sum(expo, axis=-1, keepdims=True)).astype(jnp.bfloat16)
        window_out = jnp.einsum(
            "hst,hte->hse", probs, all_values, preferred_element_type=jnp.float32
        )
        combined = (normalize(linear) + window_out).astype(jnp.bfloat16)
        new_state = state + jnp.einsum(
            "hsd,hse->hde", keys, values, preferred_element_type=jnp.float32
        )
        return (new_state, combined)

    _, outs = lax.scan(block_step, start_state, jnp.arange(block_count, dtype=jnp.int32))
    heads_out = jnp.transpose(outs, (0, 2, 1, 3)).reshape(slab_rows, inner_width)
    regrouped = lax.all_to_all(heads_out, "heads", split_axis=0, concat_axis=1, tiled=True)
    attn = jnp.dot(
        regrouped,
        lax.all_gather(w_out, "heads", axis=0, tiled=True),
        preferred_element_type=jnp.float32,
    )
    hidden_state = (tokens.astype(jnp.float32) + attn).astype(jnp.bfloat16)
    hidden_float = hidden_state.astype(jnp.float32)
    normed = normalize(hidden_float).astype(jnp.bfloat16)
    ctx_count = lax.axis_size("ctx")
    head_count = lax.axis_size("heads")
    exp_local = w_gate.shape[0]
    expert_count = exp_local * ctx_count * head_count
    top_count = expert_ids.shape[1]
    capacity = max(2, 2 * row_count * top_count // expert_count)
    devices = ctx_count * head_count
    if row_count * devices <= expert_count * capacity:
        return dense_experts(
            hidden_float, normed, w_gate, w_up, w_down, expert_ids, gate_weights, expert_count
        )
    picks = expert_ids.reshape(-1)
    onehot = (picks[:, None] == jnp.arange(expert_count, dtype=jnp.int32)[None, :]).astype(
        jnp.int32
    )
    earlier = jnp.cumsum(onehot, axis=0) - onehot
    slots = jnp.sum(onehot * earlier, axis=1)
    destination = picks * capacity + slots
    source_rows = jnp.arange(row_count * top_count, dtype=jnp.int32) // top_count
    outgoing = jnp.zeros((expert_count * capacity, model_width), jnp.bfloat16)
    outgoing = outgoing.at[destination].set(normed[source_rows])
    sendable = outgoing.reshape(expert_count, 1, capacity, model_width)
    arrived_rows = lax.all_to_all(
        sendable, ("ctx", "heads"), split_axis=0, concat_axis=1, tiled=True
    )
    e_count, n_count, c_count, d_count = arrived_rows.shape
    flat = arrived_rows.reshape(e_count, n_count * c_count, d_count)
    gate_act = jnp.einsum("erd,edf->erf", flat, w_gate, preferred_element_type=jnp.float32)
    up_act = jnp.einsum("erd,edf->erf", flat, w_up, preferred_element_type=jnp.float32)
    hid = (jax.nn.silu(gate_act) * up_act).astype(jnp.bfloat16)
    out_rows = jnp.einsum("erf,efd->erd", hid, w_down, preferred_element_type=jnp.float32)
    finished = out_rows.astype(jnp.bfloat16).reshape(e_count, n_count, c_count, d_count)
    returned = lax.all_to_all(finished, ("ctx", "heads"), split_axis=1, concat_axis=0, tiled=True)
    returned = returned.reshape(expert_count * capacity, model_width)
    picked = returned[destination].reshape(row_count, top_count, model_width).astype(jnp.float32)
    routed = jnp.sum(gate_weights[:, :, None] * picked, axis=1)
    return (hidden_float + routed).astype(jnp.bfloat16)


def solution(mesh):
    return jax.shard_map(
        on_device,
        mesh=mesh,
        in_specs=(
            P(("groups", "ctx", "heads"), None),
            P("heads", "groups", None),
            P(None, "groups", "heads"),
            P(None, None, "heads"),
            P("heads", None),
            P(("ctx", "heads"), None, None),
            P(("ctx", "heads"), None, None),
            P(("ctx", "heads"), None, None),
            P(("groups", "ctx", "heads"), None),
            P(("groups", "ctx", "heads"), None),
        ),
        out_specs=P(("groups", "ctx", "heads"), None),
        check_vma=False,
    )
```

profile of v0, /device:TPU:0, one launch (start us, length us, event | category | flops | bytes accessed | tf_op | source)
XLA Modules:
  0.0 328.5 jit_solution(8045174008604358506)
XLA Ops:
  6.5 0.7 all-gather.5.cloned.1.call-update
  7.3 0.7 all-gather.7.cloned.1.call-update
  8.0 2.6 copy.27
  10.6 46.7 %all-gather.5.cloned.1.call-done = bf16[512,2048]{1,0:T(8,128)(2,1)} async-done(((bf16[128,2048]{1,0:T(8,128)(2,1)}), bf16[512,2048]{1,0:T(8,128)(2,1)}) %all-gather.5.cloned.1.call-update) | async-done | bytes 2097168 | tf_op jit(solution)/shard_map/all_gather | solution.py:63
  57.3 3.1 convolution_convert_fusion
  60.4 0.2 convolution_convert_fusion.1
  60.6 0.7 fusion.38
  61.3 5.4 %all-gather = bf16[512,128]{1,0:T(8,128)(2,1)S(1)} all-gather(bf16[128,128]{1,0:T(8,128)(2,1)S(1)} %convolution_convert_fusion.1), channel_id=2, replica_groups=mesh['groups'=2,'ctx'=4,'heads'=4] {'ctx'}, dimensions={0}, use_global_device_ids=true | all-gather | bytes 163840 | tf_op jit(solution)/shard_map/all_gather | solution.py:13
  66.7 1.0 copy.35
  67.8 1.7 copy.34
  69.4 1.6 pad_maximum_fusion
  71.1 3.0 collective-permute-start
  74.0 2.0 fusion.26
  76.0 2.3 multiply_reduce_fusion.1
  78.3 1.1 bitcast_select_fusion
  79.4 1.5 fusion.39
  80.9 0.5 fusion.11
  81.5 0.6 fusion.15
  82.1 0.8 copy.33
  82.8 3.5 %all-to-all-start = ((bf16[4,128,128]{1,2,0:T(8,128)(2,1)}), bf16[4,128,128]{1,2,0:T(8,128)(2,1)S(1)}, u32[]{:S(2)}, u32[]{:S(2)}) async-start(bf16[4,128,128]{1,2,0:T(8,128)(2,1)} %copy.33), calls=%async_computation | async-start | bytes 262144 | tf_op jit(solution)/shard_map/all_to_all | solution.py:118
  86.3 0.0 all-gather.9.cloned.1.call-start
  86.3 19.8 %all-gather.7.cloned.1.call-done = bf16[512,2048]{1,0:T(8,128)(2,1)} async-done(((bf16[128,2048]{1,0:T(8,128)(2,1)}), bf16[512,2048]{1,0:T(8,128)(2,1)}) %all-gather.7.cloned.1.call-update) | async-done | bytes 2097168 | tf_op jit(solution)/shard_map/all_gather | solution.py:121
  106.2 2.2 multiply_reduce_fusion
  108.4 1.0 copy-done.1
  109.4 0.9 multiply_convert_fusion.2
  110.4 0.0 reduce-scatter.2.cloned.1.call-start
  110.5 33.1 %all_gather.22 = f32[2048,16]{0,1:T(8,128)S(1)} all-gather(f32[128,16]{0,1:T(8,128)S(1)} %select_reduce_fusion), channel_id=1, replica_groups=mesh['groups'=2,'ctx'=4,'heads'=4] {'ctx','heads'}, dimensions={0}, use_global_device_ids=true | all-gather | bytes 139264 | tf_op jit(solution)/shard_map/all_gather | solution.py:39
  143.6 41.7 %all-gather.9.cloned.1.call-done = bf16[2048,2048]{1,0:T(8,128)(2,1)} async-done(((bf16[128,2048]{1,0:T(8,128)(2,1)}), bf16[2048,2048]{1,0:T(8,128)(2,1)}) %all-gather.9.cloned.1.call-update) | async-done | bytes 8388624 | tf_op jit(solution)/shard_map/all_gather | solution.py:41
  185.3 11.7 %fusion.3 = f32[2048,768]{1,0:T(8,128)} fusion(bf16[2048,2048]{1,0:T(8,128)(2,1)} %all-gather.9.cloned.1.call-done, bf16[1,2048,768]{2,1,0:T(8,128)(2,1)} %param.17), kind=kOutput, calls=%fused_computation.5 | convolution fusion | flops 6442450944 | bytes 17825792 | tf_op jit(solution)/shard_map/dot_general | solution.py:44
  197.0 20.6 %multiply_convert_fusion = bf16[2048,2048]{1,0:T(8,128)(2,1)} fusion(f32[2048]{0:T(1024)S(1)} %bitcast.98, f32[2048,768]{1,0:T(8,128)} %fusion.3, bf16[2048,2048]{1,0:T(8,128)(2,1)} %all-gather.9.cloned.1.call-done, bf16[1,768,2048]{2,1,0:T(8,128)(2,1)S(1)} %copy-done, bf16[1,2048,768]{2,1,0:T(8,128)(2,1)} %param.18), kind=kOutput, calls=%fused_computation.1 | convolution fusion | flops 12902727680 | bytes 29368320 | tf_op jit(solution)/shard_map/dot_general | solution.py:47
  217.6 102.2 %reduce-scatter.2.cloned.1.call-done = bf16[128,2048]{1,0:T(8,128)(2,1)} async-done(((bf16[2048,2048]{1,0:T(8,128)(2,1)}), bf16[128,2048]{1,0:T(8,128)(2,1)}) %reduce-scatter.2.cloned.1.call-update) | async-done | bytes 524304 | tf_op jit(solution)/shard_map/reduce_scatter | solution.py:51
  319.7 2.3 add_convert_fusion
  (29 shorter events, 0.2 us)
Async XLA Ops:
  6.5 190.4 %copy-start = (bf16[1,768,2048]{2,1,0:T(8,128)(2,1)S(1)}, bf16[1,768,2048]{2,1,0:T(8,128)(2,1)}, u32[]{:S(2)}) copy-start(bf16[1,768,2048]{2,1,0:T(8,128)(2,1)} %param.19) | copy-start | bytes 9437188
  6.5 50.8 %all-gather.5.cloned.1.call-start = ((), (), s32[]{:S(2)}) async-start(), calls=%async_computation.2 | async-start | bytes 2621440 | tf_op jit(solution)/shard_map/all_gather | solution.py:63
  7.3 98.9 %all-gather.7.cloned.1.call-start = ((), (), s32[]{:S(2)}) async-start(), calls=%async_computation.3 | async-start | bytes 2621440 | tf_op jit(solution)/shard_map/all_gather | solution.py:121
  57.3 16.7 %copy-start.4 = (f32[1,128,128]{2,1,0:T(8,128)S(1)}, f32[1,128,128]{2,1,0:T(8,128)}, u32[]{:S(2)}) copy-start(f32[1,128,128]{2,1,0:T(8,128)} %param.13) | copy-start | bytes 196612
  60.4 6.3 %copy-start.3 = (bf16[512,384]{0,1:T(8,128)(2,1)}, bf16[512,384]{0,1:T(8,128)(2,1)S(1)}, u32[]{:S(2)}) copy-start(bf16[512,384]{0,1:T(8,128)(2,1)S(1)} %convolution_convert_fusion) | copy-start | bytes 1179652
  71.1 7.3 %collective-permute-start = (bf16[2,1,512,128]{3,2,1,0:T(8,128)(2,1)}, bf16[2,1,512,128]{3,2,1,0:T(8,128)(2,1)}, u32[]{:S(2)}, u32[]{:S(2)}) collective-permute-start(bf16[2,1,512,128]{3,2,1,0:T(8,128)(2,1)} %pad_maximum_fusion), channel_id=1, source_target_pairs={{0,4},{4,8},{8,12},{1,5},{5,9},{9,13},{2,6},{6,10},{10,14},{3,7},{... | collective-permute-start | bytes 786440 | tf_op jit(solution)/shard_map/ppermute | solution.py:25
  74.0 5.4 %copy-start.2 = (bf16[512,1,1,128]{3,0,2,1:T(8,128)(2,1)S(1)}, bf16[512,1,1,128]{3,0,2,1:T(8,128)(2,1)}, u32[]{:S(2)}) copy-start(bf16[512,1,1,128]{3,0,2,1:T(8,128)(2,1)} %copy.34) | copy-start | bytes 393220
  79.4 2.1 copy-start.7
  82.8 27.6 %copy-start.5 = (f32[128,8]{0,1:T(8,128)S(1)}, f32[128,8]{0,1:T(8,128)}, u32[]{:S(2)}) copy-start(f32[128,8]{0,1:T(8,128)} %param.21) | copy-start | bytes 12292
  82.8 27.6 %copy-start.6 = (s32[128,8]{0,1:T(8,128)S(1)}, s32[128,8]{0,1:T(8,128)}, u32[]{:S(2)}) copy-start(s32[128,8]{0,1:T(8,128)} %param.20) | copy-start | bytes 12292
  82.8 23.4 %all-to-all-start = ((bf16[4,128,128]{1,2,0:T(8,128)(2,1)}), bf16[4,128,128]{1,2,0:T(8,128)(2,1)S(1)}, u32[]{:S(2)}, u32[]{:S(2)}) async-start(bf16[4,128,128]{1,2,0:T(8,128)(2,1)} %copy.33), calls=%async_computation | async-start | bytes 262144 | tf_op jit(solution)/shard_map/all_to_all | solution.py:118
  86.3 99.0 %all-gather.9.cloned.1.call-start = ((), (), s32[]{:S(2)}) async-start(), calls=%async_computation.4 | async-start | bytes 8912896 | tf_op jit(solution)/shard_map/all_gather | solution.py:41
  108.4 1.0 copy-start.1
  110.4 209.4 %reduce-scatter.2.cloned.1.call-start = ((), (), s32[]{:S(2)}) async-start(), calls=%async_computation.5 | async-start | bytes 8912896 | tf_op jit(solution)/shard_map/reduce_scatter | solution.py:51
Sparse Core Ops, SparseCore 0:
  8.9 48.3 all-gather.4
  58.9 47.2 all-gather.6
  110.5 74.7 all-gather.8
  217.7 101.9 reduce-scatter.1
where the time goes:
time: 329 us
  waiting for transfers between devices  212 us (64%)
  matrix products  44.1 us (13%)
  blocking collectives  38.5 us (12%)
  between operations  13.3 us (4%)
  local copies, waits for them, and re-layouts  7.86 us (2%)
  starting transfers between devices  6.54 us (2%)
  other arithmetic  6.41 us (2%)
    reduce_scatter x1, waiting for transfers between devices, dense_experts(): lax.psum_scatter(total.astype(jnp.bfloat16), axes, scatter_dimension=0, t...  102 us
    all_gather x1, waiting for transfers between devices, on_device(): lax.all_gather(tokens, 'heads', axis=0, tiled=True)  46.7 us
    all_gather x1, waiting for transfers between devices, dense_experts(): rows = lax.all_gather(normed, axes, axis=0, tiled=True)  41.7 us
    all_gather x1, blocking collectives, dense_experts(): weights = lax.all_gather(table, axes, axis=0, tiled=True)  33.1 us
    dot_general x1, matrix products, dense_experts(): out_rows = jnp.dot(hid, w_down[e], preferred_element_type=jnp.float32)  20.6 us
    all_gather x1, waiting for transfers between devices, on_device(): lax.all_gather(w_out, 'heads', axis=0, tiled=True)  19.8 us
    dot_general x1, matrix products, dense_experts(): gate_act = jnp.dot(rows, w_gate[e], preferred_element_type=jnp.float32)  11.7 us
  transfers between devices with their start and end apart: 6, of which 4 were waited for; matrix products, arithmetic and copies ran while one was open for 6% of the time, Pallas kernels for 0%

commit v1 on v0

--- a/solution.py
+++ b/solution.py
@@ -6,6 +6,17 @@
 
 HDIM = 128
 WINDOW = 512
+
+
+def collect(array, axis, dim):
+    ways = lax.axis_size(axis)
+    pieces = [array]
+    for far in range(1, ways):
+        pieces.append(
+            lax.ppermute(pieces[far - 1], axis, [(d, (d - 1) % ways) for d in range(ways)])
+        )
+    line = jnp.concatenate(pieces, axis=dim)
+    return jnp.roll(line, lax.axis_index(axis) * array.shape[dim], axis=dim)
 
 
 def entering(x, axis, join, neutral):
@@ -116,11 +127,7 @@
     _, outs = lax.scan(block_step, start_state, jnp.arange(block_count, dtype=jnp.int32))
     heads_out = jnp.transpose(outs, (0, 2, 1, 3)).reshape(slab_rows, inner_width)
     regrouped = lax.all_to_all(heads_out, "heads", split_axis=0, concat_axis=1, tiled=True)
-    attn = jnp.dot(
-        regrouped,
-        lax.all_gather(w_out, "heads", axis=0, tiled=True),
-        preferred_element_type=jnp.float32,
-    )
+    attn = jnp.dot(regrouped, collect(w_out, "heads", 0), preferred_element_type=jnp.float32)
     hidden_state = (tokens.astype(jnp.float32) + attn).astype(jnp.bfloat16)
     hidden_float = hidden_state.astype(jnp.float32)
     normed = normalize(hidden_float).astype(jnp.bfloat16)

time: 329 us -> 347 us (1.055)
  local copies, waits for them, and re-layouts: 7.86 us -> 21.8 us
  starting transfers between devices: 6.54 us -> 17.9 us
  waiting for transfers between devices: 212 us -> 205 us
    ppermute x0 -> x3, waiting for transfers between devices: none -> 54.6 us  [collect(): lax.ppermute(pieces[far - 1], axis, [(d, (d - 1) % ways) for d in range(w...]
    all_gather x1, waiting for transfers between devices: 46.7 us -> 0.01 us  [on_device(): lax.all_gather(tokens, 'heads', axis=0, tiled=True)]
    all_gather x1 -> x0, waiting for transfers between devices: 19.8 us -> none  [on_device(): lax.all_gather(w_out, 'heads', axis=0, tiled=True)]
    unnamed x19 -> x28, local copies, waits for them, and re-layouts: 6.34 us -> 18.5 us
    ppermute x0 -> x3, starting transfers between devices: none -> 9.31 us  [collect(): lax.ppermute(pieces[far - 1], axis, [(d, (d - 1) % ways) for d in range(w...]
    all_to_all x1, waiting for transfers between devices: 0.01 us -> 4.62 us  [on_device(): lax.all_to_all(heads_out, 'heads', split_axis=0, concat_axis=1, tiled=True)]
  transfers between devices with their start and end apart: 6 -> 8, of which waited for: 4 -> 6; matrix products, arithmetic and copies ran while one was open for 6% -> 6% of each run, Pallas kernels for 0% -> 0%
where the time goes in v1:
time: 347 us; the launch traced here: 346 us
  waiting for transfers between devices  205 us (59%)
  matrix products  44.1 us (13%)
  blocking collectives  38.1 us (11%)
  local copies, waits for them, and re-layouts  21.8 us (6%)
  starting transfers between devices  17.9 us (5%)
  between operations  13.3 us (4%)
  other arithmetic  6.45 us (2%)
    reduce_scatter x1, waiting for transfers between devices, dense_experts(): lax.psum_scatter(total.astype(jnp.bfloat16), axes, scatter_dimension=0, t...  102 us
    ppermute x3, waiting for transfers between devices, collect(): lax.ppermute(pieces[far - 1], axis, [(d, (d - 1) % ways) for d in range(w...  54.6 us
    all_gather x1, waiting for transfers between devices, dense_experts(): rows = lax.all_gather(normed, axes, axis=0, tiled=True)  42.6 us
    all_gather x1, blocking collectives, dense_experts(): weights = lax.all_gather(table, axes, axis=0, tiled=True)  32.7 us
    dot_general x1, matrix products, dense_experts(): out_rows = jnp.dot(hid, w_down[e], preferred_element_type=jnp.float32)  20.6 us
    unnamed x28, local copies, waits for them, and re-layouts  18.5 us
    dot_general x1, matrix products, dense_experts(): gate_act = jnp.dot(rows, w_gate[e], preferred_element_type=jnp.float32)  11.7 us
    ppermute x3, starting transfers between devices, collect(): lax.ppermute(pieces[far - 1], axis, [(d, (d - 1) % ways) for d in range(w...  9.31 us
  transfers between devices with their start and end apart: 8, of which 6 were waited for; matrix products, arithmetic and copies ran while one was open for 6% of the time, Pallas kernels for 0%

profile of v1, /device:TPU:0, one launch (start us, length us, event | category | flops | bytes accessed | tf_op | source)
XLA Modules:
  0.0 346.3 jit_solution(7733743988309428497)
XLA Ops:
  7.3 5.1 %collective-permute-start.1 = (bf16[128,2048]{1,0:T(8,128)(2,1)}, bf16[128,2048]{1,0:T(8,128)(2,1)S(1)}, u32[]{:S(2)}, u32[]{:S(2)}) collective-permute-start(bf16[128,2048]{1,0:T(8,128)(2,1)} %param.16), channel_id=1, source_target_pairs={{0,3},{1,0},{2,1},{3,2},{4,7},{5,4},{6,5},{7,6},{8,11},{9,8},{10,9... | collective-permute-start | bytes 1572872 | tf_op jit(solution)/shard_map/ppermute | solution.py:16
  12.4 16.6 %collective-permute-done.1 = bf16[128,2048]{1,0:T(8,128)(2,1)S(1)} collective-permute-done((bf16[128,2048]{1,0:T(8,128)(2,1)}, bf16[128,2048]{1,0:T(8,128)(2,1)S(1)}, u32[]{:S(2)}, u32[]{:S(2)}) %collective-permute-start.1) | collective-permute-done | bytes 524320 | tf_op jit(solution)/shard_map/ppermute | solution.py:16
  29.7 4.2 %collective-permute-start.2 = (bf16[128,2048]{1,0:T(8,128)(2,1)S(1)}, bf16[128,2048]{1,0:T(8,128)(2,1)}, u32[]{:S(2)}, u32[]{:S(2)}) collective-permute-start(bf16[128,2048]{1,0:T(8,128)(2,1)S(1)} %collective-permute-done.1), channel_id=1, source_target_pairs={{0,3},{1,0},{2,1},{3,2},{4,7},{5,4},{6,5},{7,6},{8,11},{9,8},{10,9... | collective-permute-start | bytes 1572872 | tf_op jit(solution)/shard_map/ppermute | solution.py:16
  33.9 34.0 %collective-permute-done.2 = bf16[128,2048]{1,0:T(8,128)(2,1)} collective-permute-done((bf16[128,2048]{1,0:T(8,128)(2,1)S(1)}, bf16[128,2048]{1,0:T(8,128)(2,1)}, u32[]{:S(2)}, u32[]{:S(2)}) %collective-permute-start.2) | collective-permute-done | bytes 524320 | tf_op jit(solution)/shard_map/ppermute | solution.py:16
  67.9 1.9 constant_dynamic-update-slice_fusion.7
  69.8 2.6 copy.27
  72.4 1.9 constant_dynamic-update-slice_fusion.6
  74.4 1.9 constant_dynamic-update-slice_fusion.5
  76.3 4.0 %collective-permute-done.3 = bf16[128,2048]{1,0:T(8,128)(2,1)} collective-permute-done((bf16[128,2048]{1,0:T(8,128)(2,1)}, bf16[128,2048]{1,0:T(8,128)(2,1)}, u32[]{:S(2)}, u32[]{:S(2)}) %collective-permute-start.3) | collective-permute-done | bytes 524320 | tf_op jit(solution)/shard_map/ppermute | solution.py:16
  80.3 1.9 constant_dynamic-update-slice_fusion.4
  82.2 1.9 constant_dynamic-update-slice_fusion.3
  84.9 1.9 constant_dynamic-update-slice_fusion.1
  86.8 3.1 convolution_convert_fusion
  90.8 5.4 %all-gather = bf16[512,128]{1,0:T(8,128)(2,1)S(1)} all-gather(bf16[128,128]{1,0:T(8,128)(2,1)S(1)} %convolution_convert_fusion.1), channel_id=2, replica_groups=mesh['groups'=2,'ctx'=4,'heads'=4] {'ctx'}, dimensions={0}, use_global_device_ids=true | all-gather | bytes 163840 | tf_op jit(solution)/shard_map/all_gather | solution.py:24
  96.2 1.0 copy.35
  98.0 1.6 pad_maximum_fusion
  99.6 3.0 collective-permute-start
  102.6 1.9 fusion.27
  104.6 2.3 multiply_reduce_fusion.1
  106.9 1.1 bitcast_select_fusion
  108.0 1.5 fusion.41
  111.5 5.5 %all-to-all-start = ((bf16[4,128,128]{1,2,0:T(8,128)(2,1)}), bf16[4,128,128]{1,2,0:T(8,128)(2,1)S(1)}, u32[]{:S(2)}, u32[]{:S(2)}) async-start(bf16[4,128,128]{1,2,0:T(8,128)(2,1)} %copy.33), calls=%async_computation | async-start | bytes 262144 | tf_op jit(solution)/shard_map/all_to_all | solution.py:129
  117.0 1.9 constant_dynamic-update-slice_fusion
  118.9 4.6 %all-to-all-done = bf16[4,128,128]{1,2,0:T(8,128)(2,1)S(1)} async-done(((bf16[4,128,128]{1,2,0:T(8,128)(2,1)}), bf16[4,128,128]{1,2,0:T(8,128)(2,1)S(1)}, u32[]{:S(2)}, u32[]{:S(2)}) %all-to-all-start) | async-done | bytes 131104 | tf_op jit(solution)/shard_map/all_to_all | solution.py:129
  123.5 2.2 multiply_reduce_fusion
  125.8 1.0 copy-done.1
  127.8 32.7 %all_gather.18 = f32[2048,16]{0,1:T(8,128)S(1)} all-gather(f32[128,16]{0,1:T(8,128)S(1)} %select_reduce_fusion), channel_id=1, replica_groups=mesh['groups'=2,'ctx'=4,'heads'=4] {'ctx','heads'}, dimensions={0}, use_global_device_ids=true | all-gather | bytes 139264 | tf_op jit(solution)/shard_map/all_gather | solution.py:50
  160.4 42.6 %all-gather.6.cloned.1.call-done = bf16[2048,2048]{1,0:T(8,128)(2,1)} async-done(((bf16[128,2048]{1,0:T(8,128)(2,1)}), bf16[2048,2048]{1,0:T(8,128)(2,1)}) %all-gather.6.cloned.1.call-update) | async-done | bytes 8388624 | tf_op jit(solution)/shard_map/all_gather | solution.py:52
  203.0 11.7 %fusion.3 = f32[2048,768]{1,0:T(8,128)} fusion(bf16[2048,2048]{1,0:T(8,128)(2,1)} %all-gather.6.cloned.1.call-done, bf16[1,2048,768]{2,1,0:T(8,128)(2,1)} %param.17), kind=kOutput, calls=%fused_computation.5 | convolution fusion | flops 6442450944 | bytes 17825792 | tf_op jit(solution)/shard_map/dot_general | solution.py:55
  214.7 20.6 %multiply_convert_fusion = bf16[2048,2048]{1,0:T(8,128)(2,1)} fusion(f32[2048]{0:T(1024)S(1)} %bitcast.97, f32[2048,768]{1,0:T(8,128)} %fusion.3, bf16[2048,2048]{1,0:T(8,128)(2,1)} %all-gather.6.cloned.1.call-done, bf16[1,768,2048]{2,1,0:T(8,128)(2,1)S(1)} %copy-done, bf16[1,2048,768]{2,1,0:T(8,128)(2,1)} %param.18), kind=kOutput, calls=%fused_computation.1 | convolution fusion | flops 12902727680 | bytes 29368320 | tf_op jit(solution)/shard_map/dot_general | solution.py:58
  235.3 102.2 %reduce-scatter.2.cloned.1.call-done = bf16[128,2048]{1,0:T(8,128)(2,1)} async-done(((bf16[2048,2048]{1,0:T(8,128)(2,1)}), bf16[128,2048]{1,0:T(8,128)(2,1)}) %reduce-scatter.2.cloned.1.call-update) | async-done | bytes 524304 | tf_op jit(solution)/shard_map/reduce_scatter | solution.py:62
  337.5 2.3 add_convert_fusion
  (42 shorter events, 6.9 us)
Async XLA Ops:
  6.5 208.2 %copy-start = (bf16[1,768,2048]{2,1,0:T(8,128)(2,1)S(1)}, bf16[1,768,2048]{2,1,0:T(8,128)(2,1)}, u32[]{:S(2)}) copy-start(bf16[1,768,2048]{2,1,0:T(8,128)(2,1)} %param.19) | copy-start | bytes 9437188
  6.5 80.3 %all-gather.4.cloned.1.call-start = ((), (), s32[]{:S(2)}) async-start(), calls=%async_computation.2 | async-start | bytes 2621440 | tf_op jit(solution)/shard_map/all_gather | solution.py:74
  7.3 21.7 %collective-permute-start.1 = (bf16[128,2048]{1,0:T(8,128)(2,1)}, bf16[128,2048]{1,0:T(8,128)(2,1)S(1)}, u32[]{:S(2)}, u32[]{:S(2)}) collective-permute-start(bf16[128,2048]{1,0:T(8,128)(2,1)} %param.16), channel_id=1, source_target_pairs={{0,3},{1,0},{2,1},{3,2},{4,7},{5,4},{6,5},{7,6},{8,11},{9,8},{10,9... | collective-permute-start | bytes 1572872 | tf_op jit(solution)/shard_map/ppermute | solution.py:16
  28.9 0.8 copy-start.2
  29.7 38.2 %collective-permute-start.2 = (bf16[128,2048]{1,0:T(8,128)(2,1)S(1)}, bf16[128,2048]{1,0:T(8,128)(2,1)}, u32[]{:S(2)}, u32[]{:S(2)}) collective-permute-start(bf16[128,2048]{1,0:T(8,128)(2,1)S(1)} %collective-permute-done.1), channel_id=1, source_target_pairs={{0,3},{1,0},{2,1},{3,2},{4,7},{5,4},{6,5},{7,6},{8,11},{9,8},{10,9... | collective-permute-start | bytes 1572872 | tf_op jit(solution)/shard_map/ppermute | solution.py:16
  67.9 12.4 %collective-permute-start.3 = (bf16[128,2048]{1,0:T(8,128)(2,1)}, bf16[128,2048]{1,0:T(8,128)(2,1)}, u32[]{:S(2)}, u32[]{:S(2)}) collective-permute-start(bf16[128,2048]{1,0:T(8,128)(2,1)} %collective-permute-done.2), channel_id=1, source_target_pairs={{0,3},{1,0},{2,1},{3,2},{4,7},{5,4},{6,5},{7,6},{8,11},{9,8},{10,9... | collective-permute-start | bytes 1572872 | tf_op jit(solution)/shard_map/ppermute | solution.py:16
  72.4 11.6 %copy-start.3 = (bf16[128,2048]{1,0:T(8,128)(2,1)S(1)}, bf16[128,2048]{1,0:T(8,128)(2,1)}, u32[]{:S(2)}) copy-start(bf16[128,2048]{1,0:T(8,128)(2,1)} %copy-done.2) | copy-start | bytes 1572868
  86.8 15.8 %copy-start.5 = (f32[1,128,128]{2,1,0:T(8,128)S(1)}, f32[1,128,128]{2,1,0:T(8,128)}, u32[]{:S(2)}) copy-start(f32[1,128,128]{2,1,0:T(8,128)} %param.13) | copy-start | bytes 196612
  89.9 6.3 %copy-start.4 = (bf16[512,384]{0,1:T(8,128)(2,1)}, bf16[512,384]{0,1:T(8,128)(2,1)S(1)}, u32[]{:S(2)}) copy-start(bf16[512,384]{0,1:T(8,128)(2,1)S(1)} %convolution_convert_fusion) | copy-start | bytes 1179652
  99.6 7.3 %collective-permute-start = (bf16[2,1,512,128]{3,2,1,0:T(8,128)(2,1)}, bf16[2,1,512,128]{3,2,1,0:T(8,128)(2,1)}, u32[]{:S(2)}, u32[]{:S(2)}) collective-permute-start(bf16[2,1,512,128]{3,2,1,0:T(8,128)(2,1)} %pad_maximum_fusion), channel_id=1, source_target_pairs={{0,4},{4,8},{8,12},{1,5},{5,9},{9,13},{2,6},{6,10},{10,14},{3,7},{... | collective-permute-start | bytes 786440 | tf_op jit(solution)/shard_map/ppermute | solution.py:36
  106.9 3.2 copy-start.8
  110.7 17.1 %copy-start.6 = (f32[128,8]{0,1:T(8,128)S(1)}, f32[128,8]{0,1:T(8,128)}, u32[]{:S(2)}) copy-start(f32[128,8]{0,1:T(8,128)} %param.21) | copy-start | bytes 12292
  110.7 17.1 %copy-start.7 = (s32[128,8]{0,1:T(8,128)S(1)}, s32[128,8]{0,1:T(8,128)}, u32[]{:S(2)}) copy-start(s32[128,8]{0,1:T(8,128)} %param.20) | copy-start | bytes 12292
  111.5 12.1 %all-to-all-start = ((bf16[4,128,128]{1,2,0:T(8,128)(2,1)}), bf16[4,128,128]{1,2,0:T(8,128)(2,1)S(1)}, u32[]{:S(2)}, u32[]{:S(2)}) async-start(bf16[4,128,128]{1,2,0:T(8,128)(2,1)} %copy.33), calls=%async_computation | async-start | bytes 262144 | tf_op jit(solution)/shard_map/all_to_all | solution.py:129
  117.0 86.0 %all-gather.6.cloned.1.call-start = ((), (), s32[]{:S(2)}) async-start(), calls=%async_computation.3 | async-start | bytes 8912896 | tf_op jit(solution)/shard_map/all_gather | solution.py:52
  125.7 1.0 copy-start.1
  127.7 209.8 %reduce-scatter.2.cloned.1.call-start = ((), (), s32[]{:S(2)}) async-start(), calls=%async_computation.4 | async-start | bytes 8912896 | tf_op jit(solution)/shard_map/reduce_scatter | solution.py:62
Sparse Core Ops, SparseCore 0:
  8.9 62.7 all-gather.3
  127.8 75.1 all-gather.5
  235.4 102.0 reduce-scatter.1
